TPU v7x, 512 devices: a whole 4x8x8 slice. The times are simulated.
512 devices in a mesh: dp: 16 (over z_lo, y), mp: 8 (over z_hi, core), section: 4 (over x).
Axes of the slice: x: 4, y: 8, z: 8 (z_hi: 4, z_lo: 2; z = z_hi * 2 + z_lo), core: 2. Of those that a mesh axis runs over, the one named last changes fastest.
Arguments:
- states: bfloat16 [16384, 8192], P(('dp', 'section'), 'mp'), may hold values from -6 to 6
- direction: bfloat16 [16384, 1024], P(('dp', 'section'), 'mp'), may hold values from -0.09375 to 0.09375
- old_logp: bfloat16 [16384], P(('dp', 'section')), may hold values from -4 to -0.049804688
- lengths: int32 [128], P(('dp', 'section')), may hold values from 1 to 128, as said below
- group_ids: int32 [128], P(('dp', 'section')), may hold values from 0 to 15, as said below
- routes: int32 [16384, 1], P(('dp', 'section')), may hold values from 0 to 15; in each aligned block of 256 rows (0 to 255, 256 to 511, ...) at most 20 rows name the same one
- reward_head: bfloat16 [8192], P('mp'), may hold values from -0.0625 to 0.0625
- policy_k: bfloat16 [8192, 1024], P(('dp', 'section'), 'mp'), may hold values from -0.0625 to 0.0625
- reference_k: bfloat16 [8192, 1024], P(('dp', 'section'), 'mp'), may hold values from -0.0625 to 0.0625
Outputs:
- grad_k: float32 [8192, 1024], P(('dp', 'section'), 'mp')
- packed_logp: float32 [16, 4, 320], P('dp', 'section')
Inputs may be any that keep to these rules, and one draw needn't show every extreme that they name: `lengths`: some response has all 128 tokens valid. `group_ids`: each prompt id is held by exactly 8 responses. `routes`: among the rows of one rollout device at most 20 name the same learner shard, a bound that some block reaches of them.
All inputs are finite; a program needn't handle non-finite values.
Results may differ from a plain program's by a relative error of at most 0.004.
Values may be sent and summed in bfloat16 or wider, within the bound.
No kernel may reach another device: no remote copies, remote signals or barrier semaphores. Data moves between devices by JAX's collectives and lax.ppermute only.
A program may use at most 64 MiB of HBM per device.

v0:
```python
import jax
import jax.numpy as jnp
from jax import lax
from jax.sharding import PartitionSpec as P

GROUP = 8
kl_weight = 0.4
var_offset = 0.25


def row_slots(routes, shards, capacity):
    target = routes[:, 0]
    choose = (target[:, None] == jnp.arange(shards, dtype=jnp.int32)[None, :]).astype(jnp.int32)
    ranked = jnp.cumsum(choose, axis=0) - 1
    within = jnp.sum(ranked * choose, axis=1)
    places = target * capacity + within
    row_count = routes.shape[0]
    source = jnp.full((shards * capacity,), row_count, jnp.int32)
    return source.at[places].set(jnp.arange(row_count, dtype=jnp.int32))


def pick_rows(values, source):
    return jnp.take(values, source, axis=0, mode="fill", fill_value=0)


def advantages(scores, lengths, group_ids):
    seq_count = lengths.shape[0]
    seq_len = scores.shape[0] // seq_count
    groups = seq_count * lax.axis_size("dp") * lax.axis_size("section") // GROUP
    valid = (jnp.arange(seq_len, dtype=jnp.int32)[None, :] < lengths[:, None]).astype(jnp.float32)
    reward = jnp.sum(scores.reshape(seq_count, seq_len) * valid, axis=1) / jnp.sqrt(
        lengths.astype(jnp.float32)
    )
    member = (group_ids[:, None] == jnp.arange(groups, dtype=jnp.int32)[None, :]).astype(
        jnp.float32
    )
    totals, squares = lax.psum(
        (
            jnp.sum(member * reward[:, None], axis=0),
            jnp.sum(member * (reward * reward)[:, None], axis=0),
        ),
        ("dp", "section"),
    )
    center = totals / GROUP
    spread = squares / GROUP - center * center
    own_center = jnp.sum(member * center[None, :], axis=1)
    own_spread = jnp.sum(member * spread[None, :], axis=1)
    advantage = ((reward - own_center) / jnp.sqrt(own_spread + var_offset)).astype(jnp.bfloat16)
    return (jnp.repeat(advantage, seq_len), valid.reshape(-1))


def project(whole, policy_k, reference_k):
    return (
        jnp.dot(
            whole,
            lax.all_gather(policy_k, ("dp", "section"), axis=0, tiled=True),
            preferred_element_type=jnp.float32,
        ),
        jnp.dot(
            whole,
            lax.all_gather(reference_k, ("dp", "section"), axis=0, tiled=True),
            preferred_element_type=jnp.float32,
        ),
    )


def token_coef(dir_rows, old_rows, adv_rows, valid_rows, term_policy, term_reference):
    logp = old_rows.astype(jnp.float32) + term_policy
    coef = valid_rows * (
        -adv_rows * jnp.exp(term_policy) + kl_weight * (1.0 - jnp.exp(term_reference - term_policy))
    )
    change = (coef[:, None] * dir_rows.astype(jnp.float32)).astype(jnp.bfloat16)
    return (logp, change)


def weight_grads(whole, change):
    return lax.psum_scatter(
        lax.dot_general(
            whole, change, (((0,), (0,)), ((), ())), preferred_element_type=jnp.float32
        ),
        ("dp", "section"),
        scatter_dimension=0,
        tiled=True,
    )


def body(
    states, direction, old_logp, lengths, group_ids, routes, reward_head, policy_k, reference_k
):
    row_count = states.shape[0]
    score_part = jnp.dot(states, reward_head, preferred_element_type=jnp.float32)
    shards = lax.axis_size("dp")
    capacity = max(2, 5 * row_count // (4 * shards))
    source = row_slots(routes, shards, capacity)
    scores = lax.psum(score_part, "mp")
    adv_rows, valid_rows = advantages(scores, lengths, group_ids)
    extras = jnp.stack([old_logp, adv_rows, valid_rows.astype(jnp.bfloat16)], axis=1)
    send_states = pick_rows(states, source).reshape(shards, capacity, states.shape[1])
    send_dir = pick_rows(direction, source).reshape(shards, capacity, direction.shape[1])
    send_extras = pick_rows(extras, source).reshape(shards, capacity, 3)
    got_states, got_dir, got_extras = (
        lax.all_to_all(send_states, "dp", split_axis=0, concat_axis=0, tiled=True),
        lax.all_to_all(send_dir, "dp", split_axis=0, concat_axis=0, tiled=True),
        lax.all_to_all(send_extras, "dp", split_axis=0, concat_axis=0, tiled=True),
    )
    slot_count = shards * capacity
    learn_states = got_states.reshape(slot_count, states.shape[1])
    learn_dir = got_dir.reshape(slot_count, direction.shape[1])
    learn_extras = got_extras.reshape(slot_count, 3)
    whole = lax.all_gather(learn_states, "mp", axis=1, tiled=True)
    key_policy, key_reference = project(whole, policy_k, reference_k)
    dir_wide = learn_dir.astype(jnp.float32)
    term_policy, term_reference = lax.psum(
        (jnp.sum(dir_wide * key_policy, axis=1), jnp.sum(dir_wide * key_reference, axis=1)), "mp"
    )
    logp, change = token_coef(
        learn_dir,
        learn_extras[:, 0],
        learn_extras[:, 1].astype(jnp.float32),
        learn_extras[:, 2].astype(jnp.float32),
        term_policy,
        term_reference,
    )
    grad_k = weight_grads(whole, change)
    packed_logp = logp.reshape(1, 1, slot_count)
    return (grad_k, packed_logp)


def solution(mesh):
    return jax.shard_map(
        body,
        mesh=mesh,
        in_specs=(
            P(("dp", "section"), "mp"),
            P(("dp", "section"), "mp"),
            P(("dp", "section")),
            P(("dp", "section")),
            P(("dp", "section")),
            P(("dp", "section"), None),
            P("mp"),
            P(("dp", "section"), "mp"),
            P(("dp", "section"), "mp"),
        ),
        out_specs=(P(("dp", "section"), "mp"), P("dp", "section", None)),
        check_vma=False,
    )
```

profile of v0, /device:TPU:64, one launch (start us, length us, event | category | flops | bytes accessed | tf_op | source)
XLA Modules:
  0.0 1203.8 jit_solution(4523003245266882236)
XLA Ops:
  7.2 0.0 copy-start
  7.2 0.0 all-gather.6.cloned.1.call-start
  7.2 0.7 all-gather.6.cloned.1.call-update
  7.9 0.0 all-gather.4.cloned.1.call-start
  8.0 0.7 fusion.6
  8.6 0.6 reduce-window.6
  9.2 0.2 slice_reduce_fusion
  9.4 0.8 fusion.5
  10.2 0.7 compare_select_fusion
  10.9 1.4 scatter_custom_fusion
  12.3 0.0 copy-start.1
  12.4 2.1 gather_fusion
  14.5 0.1 gather.19
  14.6 0.1 broadcast_in_dim.52
  14.7 0.1 broadcast_select_fusion
  14.9 29.1 %all_to_all.15 = bf16[16,20,1024]{2,1,0:T(8,128)(2,1)S(1)} all-to-all(bf16[16,20,1024]{2,1,0:T(8,128)(2,1)S(1)} %broadcast_select_fusion), channel_id=1, replica_groups=mesh['dp'=16,'mp'=8,'section'=4] {'dp'}, dimensions={0} | all-to-all | bytes 1310720 | tf_op jit(solution)/shard_map/all_to_all | solution.py:102
  44.0 1.0 reshape.105
  45.0 0.0 all-gather.4.cloned.1.call-update
  45.0 0.0 all-gather.8.cloned.1.call-start
  45.0 0.7 all-gather.8.cloned.1.call-update
  45.7 1.4 gather_fusion.2
  47.2 0.8 broadcast_select_fusion.1
  47.9 6.3 all-to-all-start.2
  54.3 0.0 reduce-scatter.2.cloned.1.call-start
  54.4 0.2 fusion.16
  54.6 0.1 fusion.13
  54.7 7.0 all-to-all-done.2
  61.7 253.6 %all-gather.6.cloned.1.call-done = bf16[8192,128]{1,0:T(8,128)(2,1)} async-done(((bf16[128,128]{1,0:T(8,128)(2,1)}), bf16[8192,128]{1,0:T(8,128)(2,1)}) %all-gather.6.cloned.1.call-update) | async-done | bytes 2097168 | tf_op jit(solution)/shard_map/all_gather | solution.py:56
  315.3 65.4 %all-gather.4.cloned.1.call-done = bf16[320,8192]{1,0:T(8,128)(2,1)} async-done(((bf16[320,1024]{1,0:T(8,128)(2,1)}), bf16[320,8192]{1,0:T(8,128)(2,1)}) %all-gather.4.cloned.1.call-update) | async-done | bytes 5242896 | tf_op jit(solution)/shard_map/all_gather | solution.py:110
  380.7 4.8 fusion
  385.5 297.1 %all-gather.8.cloned.1.call-done = bf16[8192,128]{1,0:T(8,128)(2,1)} async-done(((bf16[128,128]{1,0:T(8,128)(2,1)}), bf16[8192,128]{1,0:T(8,128)(2,1)}) %all-gather.8.cloned.1.call-update) | async-done | bytes 2097168 | tf_op jit(solution)/shard_map/all_gather | solution.py:61
  682.6 4.8 fusion.1
  687.4 14.7 %all-reduce.1 = (f32[2,128]{1,0:T(2,128)S(1)}, f32[320]{0:T(512)S(1)}, f32[320]{0:T(512)S(1)}) all-reduce(f32[2,128]{1,0:T(2,128)S(1)} %bitcast.47, f32[320]{0:T(512)S(1)} %fusion.1, f32[320]{0:T(512)S(1)} %fusion), channel_id=1, replica_groups=mesh['dp'=16,'mp'=8,'section'=4] {'mp'}, use_global_device_ids=true, to_apply=%region_4.5 | all-reduce | flops 896 | bytes 7168 | tf_op jit(solution)/shard_map/psum | solution.py:95
  702.1 0.2 select_reduce_fusion.4
  702.3 0.1 select_reduce_fusion.3
  702.4 157.2 %all-reduce = (f32[16]{0:T(128)S(1)}, f32[16]{0:T(128)S(1)}) all-reduce(f32[16]{0:T(128)S(1)} %get-tuple-element.7, f32[16]{0:T(128)S(1)} %get-tuple-element.8), channel_id=1, replica_groups=mesh['dp'=16,'mp'=8,'section'=4] {'dp','section'}, use_global_device_ids=true, to_apply=%region_7.8 | all-reduce | flops 32 | bytes 256 | tf_op jit(solution)/shard_map/psum | solution.py:37
  859.6 0.2 select_reduce_fusion.2
  859.8 0.1 broadcast_bitcast_fusion
  859.9 0.1 copy.22
  860.1 1.4 gather_fusion.1
  861.5 0.1 copy.23
  861.6 0.1 gather.21
  861.7 10.8 all_to_all.16
  872.5 0.1 reshape.107
  872.7 6.5 fusion.2
  879.1 0.0 reduce-scatter.2.cloned.1.call-update
  879.1 0.6 reshape.108
  879.7 317.5 %reduce-scatter.2.cloned.1.call-done = f32[128,128]{1,0:T(8,128)} async-done(((f32[8192,128]{1,0:T(8,128)}), f32[128,128]{1,0:T(8,128)}) %reduce-scatter.2.cloned.1.call-update) | async-done | bytes 65552 | tf_op jit(solution)/shard_map/reduce_scatter | solution.py:77
  (30 shorter events, 0.2 us)
Async XLA Ops:
  7.2 5.2 copy-start
  7.2 308.1 %all-gather.6.cloned.1.call-start = ((), (), s32[]{:S(2)}) async-start(), calls=%async_computation.5 | async-start | bytes 2129920 | tf_op jit(solution)/shard_map/all_gather | solution.py:56
  7.9 372.8 %all-gather.4.cloned.1.call-start = ((), (), s32[]{:S(2)}) async-start(), calls=%async_computation.4 | async-start | bytes 5898240 | tf_op jit(solution)/shard_map/all_gather | solution.py:110
  12.3 33.4 %copy-start.1 = (bf16[256,128]{1,0:T(8,128)(2,1)S(1)}, bf16[256,128]{1,0:T(8,128)(2,1)}, u32[]{:S(2)}) copy-start(bf16[256,128]{1,0:T(8,128)(2,1)} %param.10) | copy-start | bytes 196612
  14.5 39.9 %copy-start.2 = (bf16[1024]{0:T(1024)(128)(2,1)S(1)}, bf16[1024]{0:T(1024)(128)(2,1)}, u32[]{:S(2)}) copy-start(bf16[1024]{0:T(1024)(128)(2,1)} %param.15) | copy-start | bytes 6148
  14.5 39.9 %copy-start.5 = (bf16[256]{0:T(256)(128)(2,1)S(1)}, bf16[256]{0:T(256)(128)(2,1)}, u32[]{:S(2)}) copy-start(bf16[256]{0:T(256)(128)(2,1)} %param.11) | copy-start | bytes 1540
  14.5 40.1 %copy-start.4 = (s32[2]{0:T(128)S(1)}, s32[2]{0:T(128)}, u32[]{:S(2)}) copy-start(s32[2]{0:T(128)} %param.12) | copy-start | bytes 28
  45.0 637.6 %all-gather.8.cloned.1.call-start = ((), (), s32[]{:S(2)}) async-start(), calls=%async_computation.6 | async-start | bytes 2129920 | tf_op jit(solution)/shard_map/all_gather | solution.py:61
  47.9 13.8 %all-to-all-start.2 = ((bf16[16,20,128]{2,1,0:T(8,128)(2,1)}), bf16[16,20,128]{2,1,0:T(8,128)(2,1)S(1)}, u32[]{:S(2)}, u32[]{:S(2)}) async-start(bf16[16,20,128]{2,1,0:T(8,128)(2,1)} %broadcast_select_fusion.1), calls=%async_computation.2 | async-start | bytes 196608 | tf_op jit(solution)/shard_map/all_to_all | solution.py:103
  54.3 1143.0 %reduce-scatter.2.cloned.1.call-start = ((), (), s32[]{:S(2)}) async-start(), calls=%async_computation.7 | async-start | bytes 4259840 | tf_op jit(solution)/shard_map/reduce_scatter | solution.py:77
  385.5 316.8 %copy-start.3 = (s32[2]{0:T(128)S(1)}, s32[2]{0:T(128)}, u32[]{:S(2)}) copy-start(s32[2]{0:T(128)} %param.13) | copy-start | bytes 28
Sparse Core Ops, SparseCore 0:
  10.1 305.1 all-gather.5
  317.4 63.2 all-gather.3
  382.8 299.7 all-gather.7
  879.3 317.9 reduce-scatter.1
where the time goes:
time: 1200 us
  waiting for transfers between devices  942 us (78%)
  blocking collectives  212 us (18%)
  matrix products  16.2 us (1%)
  between operations  14 us (1%)
    reduce_scatter x1, waiting for transfers between devices, weight_grads(): lax.psum_scatter(lax.dot_general(whole, change, (((0,), (0,)), ((), ())),...  318 us
    all_gather x1, waiting for transfers between devices, project(): lax.all_gather(reference_k, ('dp', 'section'), axis=0, tiled=True)  297 us
    all_gather x1, waiting for transfers between devices, project(): lax.all_gather(policy_k, ('dp', 'section'), axis=0, tiled=True)  254 us
    psum x1, blocking collectives, advantages(): lax.psum((jnp.sum(member * reward[:, None], axis=0), jnp.sum(member * (re...  157 us
    all_gather x1, waiting for transfers between devices, body(): whole = lax.all_gather(learn_states, 'mp', axis=1, tiled=True)  65.4 us
    all_to_all x1, blocking collectives, body(): lax.all_to_all(send_states, 'dp', split_axis=0, concat_axis=0, tiled=True)  29.1 us
  transfers between devices with their start and end apart: 5, of which 5 were waited for; matrix products, arithmetic and copies ran while one was open for 1% of the time, Pallas kernels for 0%

commit v1 on v0

--- a/solution.py
+++ b/solution.py
@@ -35,11 +35,14 @@
         jnp.float32
     )
     totals, squares = lax.psum(
-        (
-            jnp.sum(member * reward[:, None], axis=0),
-            jnp.sum(member * (reward * reward)[:, None], axis=0),
+        lax.psum(
+            (
+                jnp.sum(member * reward[:, None], axis=0),
+                jnp.sum(member * (reward * reward)[:, None], axis=0),
+            ),
+            "dp",
         ),
-        ("dp", "section"),
+        "section",
     )
     center = totals / GROUP
     spread = squares / GROUP - center * center

time: 1200 us -> 1090 us (0.908)
  the two profiles are of different devices: /device:TPU:64 before, /device:TPU:128 now
where the time goes in v1:
time: 1090 us
  waiting for transfers between devices  944 us (87%)
  blocking collectives  97.5 us (9%)
  matrix products  16.2 us (1%)
  between operations  14 us (1%)
    reduce_scatter x1, waiting for transfers between devices, weight_grads(): lax.psum_scatter(lax.dot_general(whole, change, (((0,), (0,)), ((), ())),...  320 us
    all_gather x1, waiting for transfers between devices, project(): lax.all_gather(reference_k, ('dp', 'section'), axis=0, tiled=True)  298 us
    all_gather x1, waiting for transfers between devices, project(): lax.all_gather(policy_k, ('dp', 'section'), axis=0, tiled=True)  253 us
    all_gather x1, waiting for transfers between devices, body(): whole = lax.all_gather(learn_states, 'mp', axis=1, tiled=True)  64.4 us
    psum x1, blocking collectives, advantages(): lax.psum((jnp.sum(member * reward[:, None], axis=0), jnp.sum(member * (re...  30.6 us
    all_to_all x1, blocking collectives, body(): lax.all_to_all(send_states, 'dp', split_axis=0, concat_axis=0, tiled=True)  30.2 us
  transfers between devices with their start and end apart: 5, of which 5 were waited for; matrix products, arithmetic and copies ran while one was open for 1% of the time, Pallas kernels for 0%

profile of v1, /device:TPU:128, one launch (start us, length us, event | category | flops | bytes accessed | tf_op | source)
XLA Modules:
  0.0 1091.2 jit_solution(8957405272188049484)
XLA Ops:
  7.2 0.0 copy-start
  7.2 0.0 all-gather.6.cloned.1.call-start
  7.2 0.7 all-gather.6.cloned.1.call-update
  7.9 0.0 all-gather.4.cloned.1.call-start
  8.0 0.7 fusion.6
  8.6 0.6 reduce-window.6
  9.2 0.2 slice_reduce_fusion
  9.4 0.8 fusion.5
  10.2 0.7 compare_select_fusion
  10.9 1.4 scatter_custom_fusion
  12.4 2.1 gather_fusion
  14.5 0.1 gather.19
  14.6 0.1 broadcast_in_dim.52
  14.7 0.1 broadcast_select_fusion
  14.9 30.2 %all_to_all.15 = bf16[16,20,1024]{2,1,0:T(8,128)(2,1)S(1)} all-to-all(bf16[16,20,1024]{2,1,0:T(8,128)(2,1)S(1)} %broadcast_select_fusion), channel_id=1, replica_groups=mesh['dp'=16,'mp'=8,'section'=4] {'dp'}, dimensions={0} | all-to-all | bytes 1310720 | tf_op jit(solution)/shard_map/all_to_all | solution.py:105
  45.1 1.0 reshape.105
  46.0 0.0 all-gather.4.cloned.1.call-update
  46.1 0.0 all-gather.8.cloned.1.call-start
  46.1 0.7 all-gather.8.cloned.1.call-update
  46.8 1.4 gather_fusion.2
  48.3 0.8 broadcast_select_fusion.1
  49.0 5.9 all-to-all-start.2
  54.9 0.0 reduce-scatter.2.cloned.1.call-start
  55.0 0.2 fusion.16
  55.2 0.1 fusion.13
  55.3 8.2 all-to-all-done.2
  63.5 252.7 %all-gather.6.cloned.1.call-done = bf16[8192,128]{1,0:T(8,128)(2,1)} async-done(((bf16[128,128]{1,0:T(8,128)(2,1)}), bf16[8192,128]{1,0:T(8,128)(2,1)}) %all-gather.6.cloned.1.call-update) | async-done | bytes 2097168 | tf_op jit(solution)/shard_map/all_gather | solution.py:59
  316.1 64.4 %all-gather.4.cloned.1.call-done = bf16[320,8192]{1,0:T(8,128)(2,1)} async-done(((bf16[320,1024]{1,0:T(8,128)(2,1)}), bf16[320,8192]{1,0:T(8,128)(2,1)}) %all-gather.4.cloned.1.call-update) | async-done | bytes 5242896 | tf_op jit(solution)/shard_map/all_gather | solution.py:113
  380.6 4.8 fusion
  385.4 297.6 %all-gather.8.cloned.1.call-done = bf16[8192,128]{1,0:T(8,128)(2,1)} async-done(((bf16[128,128]{1,0:T(8,128)(2,1)}), bf16[8192,128]{1,0:T(8,128)(2,1)}) %all-gather.8.cloned.1.call-update) | async-done | bytes 2097168 | tf_op jit(solution)/shard_map/all_gather | solution.py:64
  683.0 4.8 fusion.1
  687.8 12.6 %all-reduce.1 = (f32[2,128]{1,0:T(2,128)S(1)}, f32[320]{0:T(512)S(1)}, f32[320]{0:T(512)S(1)}) all-reduce(f32[2,128]{1,0:T(2,128)S(1)} %bitcast.47, f32[320]{0:T(512)S(1)} %fusion.1, f32[320]{0:T(512)S(1)} %fusion), channel_id=1, replica_groups=mesh['dp'=16,'mp'=8,'section'=4] {'mp'}, use_global_device_ids=true, to_apply=%region_4.5 | all-reduce | flops 896 | bytes 7168 | tf_op jit(solution)/shard_map/psum | solution.py:98
  700.4 0.2 select_reduce_fusion.4
  700.6 0.1 select_reduce_fusion.3
  700.7 30.6 %all-reduce = (f32[16]{0:T(128)S(1)}, f32[16]{0:T(128)S(1)}) all-reduce(f32[16]{0:T(128)S(1)} %get-tuple-element.7, f32[16]{0:T(128)S(1)} %get-tuple-element.8), channel_id=1, replica_groups=mesh['dp'=16,'mp'=8,'section'=4] {'dp'}, use_global_device_ids=true, to_apply=%region_7.8 | all-reduce | flops 32 | bytes 256 | tf_op jit(solution)/shard_map/psum | solution.py:38
  731.3 13.0 %all-reduce.2 = (f32[16]{0:T(128)S(1)}, f32[16]{0:T(128)S(1)}) all-reduce(f32[16]{0:T(128)S(1)} %get-tuple-element.9, f32[16]{0:T(128)S(1)} %get-tuple-element.10), channel_id=1, replica_groups=mesh['dp'=16,'mp'=8,'section'=4] {'section'}, use_global_device_ids=true, to_apply=%region_8.9 | all-reduce | flops 32 | bytes 256 | tf_op jit(solution)/shard_map/psum | solution.py:37
  744.3 0.2 select_reduce_fusion.2
  744.5 0.1 broadcast_bitcast_fusion
  744.6 0.1 copy.22
  744.8 1.4 gather_fusion.1
  746.2 0.1 copy.23
  746.3 0.1 gather.21
  746.4 11.0 %all_to_all.16 = bf16[16,20,3]{1,2,0:T(4,128)(2,1)S(1)} all-to-all(bf16[16,20,3]{1,2,0:T(4,128)(2,1)S(1)} %copy.24), channel_id=1, replica_groups=mesh['dp'=16,'mp'=8,'section'=4] {'dp'}, dimensions={0} | all-to-all | bytes 3840 | tf_op jit(solution)/shard_map/all_to_all | solution.py:107
  757.5 0.1 reshape.107
  757.6 6.5 fusion.2
  764.1 0.0 reduce-scatter.2.cloned.1.call-update
  764.1 0.6 reshape.108
  764.7 320.0 %reduce-scatter.2.cloned.1.call-done = f32[128,128]{1,0:T(8,128)} async-done(((f32[8192,128]{1,0:T(8,128)}), f32[128,128]{1,0:T(8,128)}) %reduce-scatter.2.cloned.1.call-update) | async-done | bytes 65552 | tf_op jit(solution)/shard_map/reduce_scatter | solution.py:80
  (31 shorter events, 0.3 us)
Async XLA Ops:
  7.2 5.2 copy-start
  7.2 309.0 %all-gather.6.cloned.1.call-start = ((), (), s32[]{:S(2)}) async-start(), calls=%async_computation.5 | async-start | bytes 2129920 | tf_op jit(solution)/shard_map/all_gather | solution.py:59
  7.9 372.7 %all-gather.4.cloned.1.call-start = ((), (), s32[]{:S(2)}) async-start(), calls=%async_computation.4 | async-start | bytes 5898240 | tf_op jit(solution)/shard_map/all_gather | solution.py:113
  12.3 34.5 %copy-start.1 = (bf16[256,128]{1,0:T(8,128)(2,1)S(1)}, bf16[256,128]{1,0:T(8,128)(2,1)}, u32[]{:S(2)}) copy-start(bf16[256,128]{1,0:T(8,128)(2,1)} %param.10) | copy-start | bytes 196612
  14.5 40.5 %copy-start.2 = (bf16[1024]{0:T(1024)(128)(2,1)S(1)}, bf16[1024]{0:T(1024)(128)(2,1)}, u32[]{:S(2)}) copy-start(bf16[1024]{0:T(1024)(128)(2,1)} %param.15) | copy-start | bytes 6148
  14.5 40.5 %copy-start.5 = (bf16[256]{0:T(256)(128)(2,1)S(1)}, bf16[256]{0:T(256)(128)(2,1)}, u32[]{:S(2)}) copy-start(bf16[256]{0:T(256)(128)(2,1)} %param.11) | copy-start | bytes 1540
  14.5 40.8 %copy-start.4 = (s32[2]{0:T(128)S(1)}, s32[2]{0:T(128)}, u32[]{:S(2)}) copy-start(s32[2]{0:T(128)} %param.12) | copy-start | bytes 28
  46.1 636.9 %all-gather.8.cloned.1.call-start = ((), (), s32[]{:S(2)}) async-start(), calls=%async_computation.6 | async-start | bytes 2129920 | tf_op jit(solution)/shard_map/all_gather | solution.py:64
  49.0 14.5 %all-to-all-start.2 = ((bf16[16,20,128]{2,1,0:T(8,128)(2,1)}), bf16[16,20,128]{2,1,0:T(8,128)(2,1)S(1)}, u32[]{:S(2)}, u32[]{:S(2)}) async-start(bf16[16,20,128]{2,1,0:T(8,128)(2,1)} %broadcast_select_fusion.1), calls=%async_computation.2 | async-start | bytes 196608 | tf_op jit(solution)/shard_map/all_to_all | solution.py:106
  54.9 1029.7 %reduce-scatter.2.cloned.1.call-start = ((), (), s32[]{:S(2)}) async-start(), calls=%async_computation.7 | async-start | bytes 4259840 | tf_op jit(solution)/shard_map/reduce_scatter | solution.py:80
  385.4 315.2 %copy-start.3 = (s32[2]{0:T(128)S(1)}, s32[2]{0:T(128)}, u32[]{:S(2)}) copy-start(s32[2]{0:T(128)} %param.13) | copy-start | bytes 28
Sparse Core Ops, SparseCore 0:
  10.1 305.9 all-gather.5
  318.3 62.2 all-gather.3
  382.7 300.2 all-gather.7
  764.2 320.3 reduce-scatter.1
